TPU v7x, 32 devices: a whole 2x2x4 slice. The times are simulated.
32 devices in a mesh: batch: 2 (over x), strip: 8 (over z, y), plate: 2 (over core).
Axes of the slice: x: 2, y: 2, z: 4, core: 2. Of those that a mesh axis runs over, the one named last changes fastest.
Arguments:
- fields: bfloat16 [32, 1088, 5, 1080], P(('batch', 'strip', 'plate')), parts along dimension 0, may hold values from 0.05 to 80, as said below
- flat_gain: bfloat16 [1088, 5, 1080], P('strip'), may hold values from 0.5 to 1.5
Outputs:
- corrected: bfloat16 [32, 1088, 5, 1080], P(('batch', 'strip', 'plate')), parts along dimension 0
- illumination: float32 [1088, 10, 1080], P('strip', 'batch'), parts along dimension 1
- mean_field: float32 [1088, 10, 1080], P('strip', 'batch'), parts along dimension 1
There are 2 independent parts, one for each index of `batch`. A program takes and returns all parts, laid end to end along the dimension named above; an argument that names none is the same for every part. Nothing has to cross between parts.
Inputs may be any that keep to these rules, and one draw needn't show every extreme that they name: `fields`: positive intensities.
All inputs are finite; a program needn't handle non-finite values.
Results may differ from a plain program's by a relative error of at most 0.0004.
The roundings to bfloat16 on the way count: a program that leaves them out, or rounds other values in their place, can miss the bound.
Values may be sent and summed in bfloat16 or wider, within the bound.
A program may use at most 192 MiB of HBM per device.

v0:
```python
import jax
import jax.numpy as jnp
from jax import lax
from jax.sharding import PartitionSpec as P

SIGMA = 16
RADIUS = 48


def padded_2(array, sides, width):
    for axis, dim in sides:
        count, length = (lax.axis_size(axis), array.shape[dim])
        up = [(i, (i + 1) % count) for i in range(count - 1)]
        down = [(j, i) for i, j in up]
        last = lax.slice_in_dim(array, length - width, length, axis=dim)
        first = lax.slice_in_dim(array, 0, width, axis=dim)
        before = lax.ppermute(last, axis, up)
        after = lax.ppermute(first, axis, down)
        array = jnp.concatenate([before, array, after], axis=dim)
    return array


def gauss_weights(out_index, in_index, length):
    offset = out_index[:, None] - in_index[None, :]
    inside = (jnp.abs(offset) <= RADIUS) & (in_index[None, :] >= 0.0) & (in_index[None, :] < length)
    weights = jnp.where(inside, jnp.exp(-offset * offset / (2.0 * SIGMA * SIGMA)), 0.0)
    return weights / jnp.sum(weights, axis=1, keepdims=True)


def on_device(fields, flat_gain):
    num_fields, height, channels, width = fields.shape
    strips = lax.axis_size("strip")
    plates = lax.axis_size("plate")
    strip_rows = height // strips
    count = num_fields * strips * plates
    block = fields
    partial_sum = lax.psum_scatter(
        jnp.sum(block, axis=0, dtype=jnp.float32), "strip", scatter_dimension=0, tiled=True
    )
    total = lax.psum(partial_sum, "plate")
    mean_field = total / count
    col_index = jnp.arange(width, dtype=jnp.float32)
    col_kernel = gauss_weights(col_index, col_index, float(width))
    smooth_cols = jnp.einsum("hcv,wv->hcw", mean_field, col_kernel, precision=lax.Precision.HIGHEST)
    padded = padded_2(smooth_cols, (("strip", 0),), RADIUS)
    first_row = (lax.axis_index("strip") * strip_rows).astype(jnp.float32)
    out_index = first_row + jnp.arange(strip_rows, dtype=jnp.float32)
    in_index = first_row - RADIUS + jnp.arange(strip_rows + 2 * RADIUS, dtype=jnp.float32)
    row_kernel = gauss_weights(out_index, in_index, float(height))
    illumination = jnp.einsum("hu,ucw->hcw", row_kernel, padded, precision=lax.Precision.HIGHEST)
    illum_round = (illumination * flat_gain.astype(jnp.float32)).astype(jnp.bfloat16)
    block = fields
    corrected = (
        block.astype(jnp.float32)
        / lax.all_gather(illum_round, "strip", axis=0, tiled=True).astype(jnp.float32)[None]
    ).astype(jnp.bfloat16)
    return (corrected, illumination, mean_field)


def solution(mesh):
    return jax.shard_map(
        on_device,
        mesh=mesh,
        in_specs=(P(("batch", "strip", "plate"), None, None, None), P("strip", None, None)),
        out_specs=(
            P(("batch", "strip", "plate"), None, None, None),
            P("strip", "batch", None),
            P("strip", "batch", None),
        ),
        check_vma=False,
    )
```

profile of v0, /device:TPU:0, one launch (start us, length us, event | category | flops | bytes accessed | tf_op | source)
XLA Modules:
  0.0 768.9 jit_solution(5044479975014153405)
XLA Ops:
  7.2 0.0 reduce-scatter.2.cloned.1.call-start
  7.2 20.2 %copy.5 = bf16[1,1088,5,1080]{3,1,2,0:T(8,128)(2,1)} copy(bf16[1,1088,5,1080]{1,3,2,0:T(8,128)(2,1)} %param.2) | data formatting | bytes 23500800 | tf_op args[0]
  27.4 14.3 %convert_bitcast_fusion = f32[1088,5,1080]{2,0,1:T(8,128)} fusion(bf16[1,1088,5,1080]{3,1,2,0:T(8,128)(2,1)} %copy.5), kind=kLoop, calls=%fused_computation.1 | loop fusion | flops 5875200 | bytes 35251200 | tf_op jit(solution)/shard_map/reduce_sum | solution.py:38
  41.7 0.0 reduce-scatter.2.cloned.1.call-update
  41.7 0.0 all-reduce.2.cloned.1.call-start
  41.7 404.8 %reduce-scatter.2.cloned.1.call-done = f32[136,5,1080]{2,0,1:T(8,128)} async-done(((f32[1088,5,1080]{2,0,1:T(8,128)}), f32[136,5,1080]{2,0,1:T(8,128)}) %reduce-scatter.2.cloned.1.call-update) | async-done | bytes 2937616 | tf_op jit(solution)/shard_map/reduce_scatter | solution.py:37
  446.5 0.0 all-reduce.2.cloned.1.call-update
  446.5 0.0 all-gather.2.cloned.1.call-start
  446.6 2.3 fusion.14
  448.9 22.2 %all-reduce.2.cloned.1.call-done = f32[136,5,1080]{2,0,1:T(8,128)} async-done(((f32[136,5,1080]{2,0,1:T(8,128)}), f32[136,5,1080]{2,0,1:T(8,128)}) %all-reduce.2.cloned.1.call-update) | async-done | bytes 2937616 | tf_op jit(solution)/shard_map/psum | solution.py:40
  471.2 2.1 broadcast_multiply_fusion
  473.3 0.0 copy-start
  473.3 15.6 %fusion.10 = f32[136,5,1080]{2,0,1:T(8,128)S(1)} fusion(f32[136,5,1080]{2,0,1:T(8,128)S(1)} %broadcast_multiply_fusion, f32[1080]{0:T(1024)S(1)} %fusion.14, pred[1080]{0:T(1024)(128)(4,1)S(1)} %iota_compare_fusion), kind=kOutput, calls=%fused_computation.13 | convolution fusion | flops 9528322048 | bytes 5880600 | tf_op jit(solution)/shard_map/hcv,wv->hcw/dot_general | solution.py:44
  488.9 0.0 copy-done
  488.9 1.5 fusion.49
  490.4 1.3 collective-permute-start.1
  491.7 5.6 collective-permute-start
  497.3 0.2 fusion.31
  497.5 21.7 %collective-permute-done.1 = f32[48,5,1080]{2,0,1:T(8,128)} collective-permute-done((f32[48,5,1080]{2,0,1:T(8,128)}, f32[48,5,1080]{2,0,1:T(8,128)}, u32[]{:S(2)}, u32[]{:S(2)}) %collective-permute-start.1) | collective-permute-done | bytes 1036832 | tf_op jit(solution)/shard_map/ppermute | solution.py:18
  519.2 23.9 %collective-permute-done = f32[48,5,1080]{2,0,1:T(8,128)} collective-permute-done((f32[48,5,1080]{2,0,1:T(8,128)}, f32[48,5,1080]{2,0,1:T(8,128)}, u32[]{:S(2)}, u32[]{:S(2)}) %collective-permute-start) | collective-permute-done | bytes 1036832 | tf_op jit(solution)/shard_map/ppermute | solution.py:17
  543.1 7.7 %multiply_convert_fusion = (bf16[136,5,1080]{2,0,1:T(8,128)(2,1)}, f32[136,5,1080]{2,0,1:T(8,128)}) fusion(bf16[136,5,1080]{2,0,1:T(8,128)(2,1)} %param.3, f32[48,5,1080]{2,0,1:T(8,128)} %collective-permute-done.1, f32[136,5,1080]{2,0,1:T(8,128)S(1)} %fusion.10, f32[48,5,1080]{2,0,1:T(8,128)} %collective-permute-done, f32[136]{0:T(256)S(1)} %fusion.31, ...), kind=kOutput, calls=%fused_computation.20 | convolution fusion | flops 2049593856 | bytes 10888880 | tf_op jit(solution)/shard_map/hu,ucw->hcw/dot_general | solution.py:50
  550.8 0.0 all-gather.2.cloned.1.call-update
  550.8 177.0 %all-gather.2.cloned.1.call-done = bf16[1088,5,1080]{2,0,1:T(8,128)(2,1)} async-done(((bf16[136,5,1080]{2,0,1:T(8,128)(2,1)}), bf16[1088,5,1080]{2,0,1:T(8,128)(2,1)}) %all-gather.2.cloned.1.call-update) | async-done | bytes 11750416 | tf_op jit(solution)/shard_map/all_gather | solution.py:55
  727.8 14.9 %fusion = bf16[1,1088,5,1080]{3,1,2,0:T(8,128)(2,1)} fusion(bf16[1,1088,5,1080]{3,1,2,0:T(8,128)(2,1)} %copy.5, bf16[1088,5,1080]{2,0,1:T(8,128)(2,1)} %all-gather.2.cloned.1.call-done), kind=kLoop, calls=%fused_computation.2 | loop fusion | flops 23500800 | bytes 35251200 | tf_op jit(solution)/shard_map/convert_element_type | solution.py:56
  742.8 19.6 %copy.6 = bf16[1,1088,5,1080]{1,3,2,0:T(8,128)(2,1)} copy(bf16[1,1088,5,1080]{3,1,2,0:T(8,128)(2,1)} %fusion) | data formatting | bytes 23500800
  (4 shorter events, 0.0 us)
Async XLA Ops:
  7.2 439.4 %reduce-scatter.2.cloned.1.call-start = ((), (), s32[]{:S(2)}) async-start(), calls=%async_computation.1 | async-start | bytes 28200960 | tf_op jit(solution)/shard_map/reduce_scatter | solution.py:37
  41.7 429.5 %all-reduce.2.cloned.1.call-start = ((), (), s32[]{:S(2)}) async-start(), calls=%async_computation.2 | async-start | bytes 6266880 | tf_op jit(solution)/shard_map/psum | solution.py:40
  446.5 281.3 %all-gather.2.cloned.1.call-start = ((), (), s32[]{:S(2)}) async-start(), calls=%async_computation.3 | async-start | bytes 14100480 | tf_op jit(solution)/shard_map/all_gather | solution.py:55
  473.3 15.6 %copy-start = (f32[136,5,1080]{2,0,1:T(8,128)}, f32[136,5,1080]{2,0,1:T(8,128)S(1)}, u32[]{:S(2)}) copy-start(f32[136,5,1080]{2,0,1:T(8,128)S(1)} %broadcast_multiply_fusion) | copy-start | bytes 8812804
  490.4 28.8 %collective-permute-start.1 = (f32[48,5,1080]{2,0,1:T(8,128)}, f32[48,5,1080]{2,0,1:T(8,128)}, u32[]{:S(2)}, u32[]{:S(2)}) collective-permute-start(f32[48,5,1080]{2,0,1:T(8,128)} %get-tuple-element.7), channel_id=1, source_target_pairs={{2,0},{4,2},{6,4},{8,6},{10,8},{12,10},{14,12},{3,1},{5,3},{7,5},{... | collective-permute-start | bytes 3110408 | tf_op jit(solution)/shard_map/ppermute | solution.py:18
  491.7 51.4 %collective-permute-start = (f32[48,5,1080]{2,0,1:T(8,128)}, f32[48,5,1080]{2,0,1:T(8,128)}, u32[]{:S(2)}, u32[]{:S(2)}) collective-permute-start(f32[48,5,1080]{2,0,1:T(8,128)} %get-tuple-element.6), channel_id=1, source_target_pairs={{0,2},{2,4},{4,6},{6,8},{8,10},{10,12},{12,14},{1,3},{3,5},{5,7},{... | collective-permute-start | bytes 3110408 | tf_op jit(solution)/shard_map/ppermute | solution.py:17
Sparse Core Ops, SparseCore 0:
  41.8 404.6 reduce-scatter.1
  448.9 22.2 all-reduce.1
  551.0 176.8 all-gather.1
where the time goes:
time: 770 us; the launch traced here: 769 us
  waiting for transfers between devices  650 us (84%)
  local copies, waits for them, and re-layouts  41.3 us (5%)
  other arithmetic  33.9 us (4%)
  matrix products  23.4 us (3%)
  between operations  13.8 us (2%)
    reduce_scatter x1, waiting for transfers between devices, on_device(): lax.psum_scatter(jnp.sum(block, axis=0, dtype=jnp.float32), 'strip', scat...  405 us
    all_gather x1, waiting for transfers between devices, on_device(): lax.all_gather(illum_round, 'strip', axis=0, tiled=True).astype(jnp.float32)  177 us
    unnamed x4, local copies, waits for them, and re-layouts  39.8 us
    ppermute x1, waiting for transfers between devices, padded_2(): before = lax.ppermute(last, axis, up)  23.9 us
    psum x1, waiting for transfers between devices, on_device(): total = lax.psum(partial_sum, 'plate')  22.2 us
    ppermute x1, waiting for transfers between devices, padded_2(): after = lax.ppermute(first, axis, down)  21.7 us
    dot_general x1, matrix products, on_device(): jnp.einsum('hcv,wv->hcw', mean_field, col_kernel, precision=lax.Precision...  15.6 us
  transfers between devices with their start and end apart: 5, of which 5 were waited for; matrix products, arithmetic and copies ran while one was open for 0% of the time, Pallas kernels for 0%

commit v1 on v0

--- a/solution.py
+++ b/solution.py
@@ -1,10 +1,29 @@
+import functools
 import jax
 import jax.numpy as jnp
 from jax import lax
+from jax.experimental import pallas as pl
+from jax.experimental.pallas import tpu as pltpu
 from jax.sharding import PartitionSpec as P
 
 SIGMA = 16
 RADIUS = 48
+ROWS = 8
+MESH = pl.DeviceIdType.MESH
+LINK = jnp.bfloat16
+
+
+def coded(mean):
+    for _ in range(4):
+        mean = mean * mean
+    return mean.astype(LINK)
+
+
+def decoded(code):
+    code = code.astype(jnp.float32)
+    for _ in range(4):
+        code = lax.rsqrt(code)
+    return code
 
 
 def padded_2(array, sides, width):
@@ -25,6 +44,290 @@
     inside = (jnp.abs(offset) <= RADIUS) & (in_index[None, :] >= 0.0) & (in_index[None, :] < length)
     weights = jnp.where(inside, jnp.exp(-offset * offset / (2.0 * SIGMA * SIGMA)), 0.0)
     return weights / jnp.sum(weights, axis=1, keepdims=True)
+
+
+def where_am_i():
+    strip, plate = lax.axis_index("strip"), lax.axis_index("plate")
+    return strip, plate, lax.rem(strip, 2), lax.div(strip, 2)
+
+
+def at(strip, plate):
+    return {"strip": strip, "plate": plate}
+
+
+def greet(nz, strip, plate, y, z):
+    barrier = pltpu.get_barrier_semaphore()
+    partners = [at(strip, 1 - plate), at(z * 2 + 1 - y, plate)]
+    partners += [at(lax.rem(z + d, nz) * 2 + y, plate) for d in range(1, nz)]
+    for partner in partners:
+        pl.semaphore_signal(barrier, inc=1, device_id=partner, device_id_type=MESH)
+    pl.semaphore_wait(barrier, len(partners))
+
+
+def reduce_kernel(x_ref, out_ref, mine, sib, pair, ybuf, zsend, zbuf, total,
+                  load_sem, sib_send, sib_recv, y_send, y_recv, z_send, z_recv, t_send, t_recv, o_sem):
+    channels, nz, _, rows, _ = x_ref.shape
+    strip, plate, y, z = where_am_i()
+    active = y == plate
+    sibling = at(strip, 1 - plate)
+    greet(nz, strip, plate, y, z)
+
+    def load(c):
+        return pltpu.make_async_copy(x_ref.at[c, :, plate], mine.at[c], load_sem.at[c])
+
+    def to_sibling(c):
+        return pltpu.make_async_remote_copy(
+            x_ref.at[c, :, 1 - plate], sib.at[c], sib_send.at[c], sib_recv.at[c],
+            device_id=sibling, device_id_type=MESH)
+
+    def across(c):
+        return pltpu.make_async_remote_copy(
+            pair.at[c], ybuf.at[c], y_send.at[c], y_recv.at[c],
+            device_id=at(z * 2 + 1 - y, plate), device_id_type=MESH)
+
+    def along(c, d):
+        return pltpu.make_async_remote_copy(
+            zsend.at[c, d], zbuf.at[c, d], z_send.at[c, d], z_recv.at[c, d],
+            device_id=at(lax.rem(z + d, nz) * 2 + y, plate), device_id_type=MESH)
+
+    def share(c):
+        return pltpu.make_async_remote_copy(
+            total.at[c], total.at[c], t_send.at[c], t_recv.at[c],
+            device_id=sibling, device_id_type=MESH)
+
+    def store(c):
+        return pltpu.make_async_copy(total.at[c], out_ref.at[c], o_sem.at[c])
+
+    @pl.loop(0, channels)
+    def _(c):
+        load(c).start()
+        to_sibling(c).start()
+
+    @pl.loop(0, channels)
+    def _(c):
+        load(c).wait()
+        to_sibling(c).wait_recv()
+
+        @pl.when(jnp.logical_not(active))
+        def _():
+            @pl.loop(0, nz)
+            def _(k):
+                for r in range(0, rows, ROWS):
+                    at_r = pl.ds(r, ROWS)
+                    value = mine[c, k, at_r, :].astype(jnp.float32) + sib[c, k, at_r, :].astype(jnp.float32)
+                    pair[c, k, at_r, :] = coded(value * 0.5)
+
+            across(c).start()
+
+    @pl.when(active)
+    def _():
+        @pl.loop(0, channels)
+        def _(c):
+            across(c).wait_recv()
+
+            def summed(k, r):
+                at_r = pl.ds(r, ROWS)
+                value = mine[c, k, at_r, :].astype(jnp.float32) + sib[c, k, at_r, :].astype(jnp.float32)
+                return value + 2.0 * decoded(ybuf[c, k, at_r, :])
+
+            @pl.loop(1, nz)
+            def _(d):
+                k = lax.rem(z + d, nz)
+                for r in range(0, rows, ROWS):
+                    zsend[c, d, pl.ds(r, ROWS), :] = coded(summed(k, r) * 0.25)
+                along(c, d).start()
+
+            for r in range(0, rows, ROWS):
+                total[c, pl.ds(r, ROWS), :] = summed(z, r)
+
+        @pl.loop(0, channels)
+        def _(c):
+            @pl.loop(1, nz)
+            def _(d):
+                along(c, d).wait_recv()
+
+            for r in range(0, rows, ROWS):
+                at_r = pl.ds(r, ROWS)
+                value = total[c, at_r, :]
+                for d in range(1, nz):
+                    value = value + 4.0 * decoded(zbuf[c, d, at_r, :])
+                total[c, at_r, :] = value
+            share(c).start()
+            store(c).start()
+
+        @pl.loop(0, channels)
+        def _(c):
+            share(c).wait_send()
+
+            @pl.loop(1, nz)
+            def _(d):
+                along(c, d).wait_send()
+
+    @pl.when(jnp.logical_not(active))
+    def _():
+        @pl.loop(0, channels)
+        def _(c):
+            share(c).wait_recv()
+            store(c).start()
+            across(c).wait_send()
+
+    @pl.loop(0, channels)
+    def _(c):
+        to_sibling(c).wait_send()
+        store(c).wait()
+
+
+def strip_totals(x):
+    channels, nz, _, rows, width = x.shape
+    part = (channels, nz, rows, width)
+    dma = pltpu.SemaphoreType.DMA
+    return pl.pallas_call(
+        reduce_kernel,
+        out_shape=jax.ShapeDtypeStruct((channels, rows, width), jnp.float32),
+        in_specs=[pl.BlockSpec(memory_space=pl.ANY)],
+        out_specs=pl.BlockSpec(memory_space=pl.ANY),
+        scratch_shapes=[
+            pltpu.VMEM(part, x.dtype), pltpu.VMEM(part, x.dtype),
+            pltpu.VMEM(part, LINK), pltpu.VMEM(part, LINK),
+            pltpu.VMEM(part, LINK), pltpu.VMEM(part, LINK),
+            pltpu.VMEM((channels, rows, width), jnp.float32),
+            dma((channels,)), dma((channels,)), dma((channels,)), dma((channels,)), dma((channels,)),
+            dma((channels, nz)), dma((channels, nz)), dma((channels,)), dma((channels,)), dma((channels,)),
+        ],
+        compiler_params=pltpu.CompilerParams(
+            collective_id=0, has_side_effects=True, vmem_limit_bytes=56 * 2**20),
+        name="strip_totals",
+    )(x)
+
+
+def gather_kernel(own_ref, out_ref, own_sem, recv_sem, send_sem):
+    channels, nz = out_ref.shape[:2]
+    strip, plate, y, z = where_am_i()
+    active = y == plate
+    greet(nz, strip, plate, y, z)
+    sibling, across = at(strip, 1 - plate), at(z * 2 + 1 - y, plate)
+    above, below = at((z + 1) * 2 + y, plate), at((z - 1) * 2 + y, plate)
+
+    def own(c):
+        return pltpu.make_async_copy(own_ref.at[c], out_ref.at[c, z, y], own_sem.at[c])
+
+    def send(c, k, column, kind, target, src=None):
+        slot = out_ref.at[c, k, column]
+        return pltpu.make_async_remote_copy(
+            slot if src is None else src, slot, send_sem.at[c, k, kind], recv_sem.at[c, k, column],
+            device_id=target, device_id_type=MESH)
+
+    def sides(d, up, down):
+        pl.when(z - d >= 0)(lambda: up(z - d))
+        pl.when(z + d < nz)(lambda: down(z + d))
+
+    @pl.when(active)
+    def _():
+        @pl.loop(0, channels)
+        def _(c):
+            own(c).start()
+            pl.when(z + 1 < nz)(lambda: send(c, z, y, 2, above, own_ref.at[c]).start())
+            pl.when(z >= 1)(lambda: send(c, z, y, 3, below, own_ref.at[c]).start())
+            send(c, z, y, 1, across, own_ref.at[c]).start()
+            send(c, z, y, 0, sibling, own_ref.at[c]).start()
+
+        @pl.loop(1, nz)
+        def _(d):
+            @pl.loop(0, channels)
+            def _(c):
+                def up(k):
+                    send(c, k, y, 2, above).wait_recv()
+                    pl.when(z + 1 < nz)(lambda: send(c, k, y, 2, above).start())
+                    send(c, k, y, 1, across).start()
+                    send(c, k, y, 0, sibling).start()
+
+                def down(k):
+                    send(c, k, y, 3, below).wait_recv()
+                    pl.when(z >= 1)(lambda: send(c, k, y, 3, below).start())
+                    send(c, k, y, 1, across).start()
+                    send(c, k, y, 0, sibling).start()
+
+                sides(d, up, down)
+
+        @pl.loop(0, channels)
+        def _(c):
+            own(c).wait()
+
+            @pl.loop(0, nz)
+            def _(k):
+                send(c, k, 1 - y, 0, sibling).wait_recv()
+                send(c, k, y, 0, sibling).wait_send()
+                send(c, k, y, 1, across).wait_send()
+                pl.when((k <= z) & (z + 1 < nz))(lambda: send(c, k, y, 2, above).wait_send())
+                pl.when((k >= z) & (z >= 1))(lambda: send(c, k, y, 3, below).wait_send())
+
+    @pl.when(jnp.logical_not(active))
+    def _():
+        @pl.loop(0, nz)
+        def _(d):
+            @pl.loop(0, channels)
+            def _(c):
+                def relay(k):
+                    send(c, k, 1 - y, 0, sibling).wait_recv()
+                    send(c, k, 1 - y, 0, sibling).start()
+
+                pl.when(z - d >= 0)(lambda: relay(z - d))
+                pl.when((z + d < nz) & (d > 0))(lambda: relay(z + d))
+
+        @pl.loop(0, channels)
+        def _(c):
+            @pl.loop(0, nz)
+            def _(k):
+                send(c, k, y, 0, sibling).wait_recv()
+                send(c, k, 1 - y, 0, sibling).wait_send()
+
+
+def gathered(own, nz):
+    channels, rows, width = own.shape
+    dma = pltpu.SemaphoreType.DMA
+    return pl.pallas_call(
+        gather_kernel,
+        out_shape=jax.ShapeDtypeStruct((channels, nz, 2, rows, width), own.dtype),
+        in_specs=[pl.BlockSpec(memory_space=pl.ANY)],
+        out_specs=pl.BlockSpec(memory_space=pl.ANY),
+        scratch_shapes=[dma((channels,)), dma((channels, nz, 2)), dma((channels, nz, 4))],
+        compiler_params=pltpu.CompilerParams(collective_id=1, has_side_effects=True),
+        name="gathered",
+    )(own)
+
+
+def on_grid(fields, flat_gain):
+    _, height, channels, width = fields.shape
+    strips = lax.axis_size("strip")
+    nz = strips // 2
+    strip_rows = height // strips
+    both = ("strip", "plate")
+    x = jnp.transpose(fields[0], (1, 0, 2))
+    total = strip_totals(x.reshape(channels, nz, 2, strip_rows, width))
+    mean_field = total / (strips * 2)
+    col_index = jnp.arange(width, dtype=jnp.float32)
+    col_kernel = gauss_weights(col_index, col_index, float(width))
+    smooth_cols = jnp.einsum("chv,wv->chw", mean_field, col_kernel, precision=lax.Precision.HIGHEST)
+    up = [(i * 2 + i % 2, (i + 1) * 2 + (i + 1) % 2) for i in range(strips - 1)]
+    down = [(j, i) for i, j in up]
+    before = lax.ppermute(smooth_cols[:, strip_rows - RADIUS:], both, up)
+    after = lax.ppermute(smooth_cols[:, :RADIUS], both, down)
+    padded = jnp.concatenate([before, smooth_cols, after], axis=1)
+    strip = lax.axis_index("strip")
+    first_row = (strip * strip_rows).astype(jnp.float32)
+    out_index = first_row + jnp.arange(strip_rows, dtype=jnp.float32)
+    in_index = first_row - RADIUS + jnp.arange(strip_rows + 2 * RADIUS, dtype=jnp.float32)
+    row_kernel = gauss_weights(out_index, in_index, float(height))
+    illumination = jnp.einsum("hu,cuw->chw", row_kernel, padded, precision=lax.Precision.HIGHEST)
+    gain = jnp.transpose(flat_gain, (1, 0, 2)).astype(jnp.float32)
+    illum_round = (illumination * gain).astype(jnp.bfloat16)
+    everywhere = gathered(illum_round, nz).reshape(channels, height, width)
+    twins = [(i * 2 + i % 2, i * 2 + 1 - i % 2) for i in range(strips)]
+    twin = lax.ppermute(illumination, both, twins)
+    illumination = jnp.where(lax.rem(strip, 2) == lax.axis_index("plate"), illumination, twin)
+    corrected = (x.astype(jnp.float32) / everywhere.astype(jnp.float32)).astype(jnp.bfloat16)
+    back = lambda a: jnp.transpose(a, (1, 0, 2))
+    return (back(corrected)[None], back(illumination), back(mean_field))
 
 
 def on_device(fields, flat_gain):
@@ -58,8 +361,9 @@
 
 
 def solution(mesh):
+    grid = mesh.shape["strip"] == 8 and mesh.shape["plate"] == 2
     return jax.shard_map(
-        on_device,
+        on_grid if grid else on_device,
         mesh=mesh,
         in_specs=(P(("batch", "strip", "plate"), None, None, None), P("strip", None, None)),
         out_specs=(

time: 770 us -> 324 us (0.42)
  waiting for transfers between devices: 650 us -> 24.6 us
  Pallas kernels: 0 us -> 173 us
  between operations: 13.8 us -> 0.7 us
  local copies, waits for them, and re-layouts: 41.3 us -> 49.5 us
    reduce_scatter x1 -> x0, waiting for transfers between devices: 405 us -> none  [on_device(): lax.psum_scatter(jnp.sum(block, axis=0, dtype=jnp.float32), 'strip', scat...]
    all_gather x1 -> x0, waiting for transfers between devices: 177 us -> none  [on_device(): lax.all_gather(illum_round, 'strip', axis=0, tiled=True).astype(jnp.float32)]
    pallas_call x0 -> x2, Pallas kernels: none -> 173 us  [the longest x1 94.9 us: strip_totals(): pl.pallas_call(reduce_kernel, out_shape=jax.ShapeDtypeStruct((channels, r...]
    unnamed x4 -> x6, local copies, waits for them, and re-layouts: 39.8 us -> 1.66 us
    convert_element_type x0 -> x1, local copies, waits for them, and re-layouts: none -> 26.2 us  [on_grid(): everywhere.astype(jnp.float32)]
    psum x1 -> x0, waiting for transfers between devices: 22.2 us -> none  [on_device(): total = lax.psum(partial_sum, 'plate')]
    ppermute x2 -> x3, waiting for transfers between devices: 45.5 us -> 24.6 us  [the longest x1 22.5 us: on_grid(): before = lax.ppermute(smooth_cols[:, strip_rows - RADIUS:], both, up)]
    transpose x0 -> x1, local copies, waits for them, and re-layouts: none -> 20.2 us  [on_grid(): x = jnp.transpose(fields[0], (1, 0, 2))]
  transfers between devices with their start and end apart: 5 -> 3, of which waited for: 5 -> 2; matrix products, arithmetic and copies ran while one was open for 0% -> 1% of each run, Pallas kernels for 0% -> 0%
where the time goes in v1:
time: 324 us; the launch traced here: 322 us
  Pallas kernels  173 us (53%)
  local copies, waits for them, and re-layouts  49.5 us (15%)
  other arithmetic  41.1 us (13%)
  matrix products  25.5 us (8%)
  waiting for transfers between devices  24.6 us (8%)
  starting transfers between devices  6.92 us (2%)
    pallas_call x1, Pallas kernels, strip_totals(): pl.pallas_call(reduce_kernel, out_shape=jax.ShapeDtypeStruct((channels, r...  94.9 us
    pallas_call x1, Pallas kernels, gathered(): pl.pallas_call(gather_kernel, out_shape=jax.ShapeDtypeStruct((channels, n...  78.6 us
    convert_element_type x1, local copies, waits for them, and re-layouts, on_grid(): everywhere.astype(jnp.float32)  26.2 us
    ppermute x1, waiting for transfers between devices, on_grid(): before = lax.ppermute(smooth_cols[:, strip_rows - RADIUS:], both, up)  22.5 us
    transpose x1, local copies, waits for them, and re-layouts, on_grid(): x = jnp.transpose(fields[0], (1, 0, 2))  20.2 us
    broadcast_in_dim x1, other arithmetic, on_grid(): return (back(corrected)[None], back(illumination), back(mean_field))  17.8 us
    dot_general x1, matrix products, on_grid(): jnp.einsum('chv,wv->chw', mean_field, col_kernel, precision=lax.Precision...  17.7 us
    convert_element_type x1, other arithmetic, on_grid(): everywhere.astype(jnp.float32)  14.3 us
  transfers between devices with their start and end apart: 3, of which 2 were waited for; matrix products, arithmetic and copies ran while one was open for 1% of the time, Pallas kernels for 0%

profile of v1, /device:TPU:0, one launch (start us, length us, event | category | flops | bytes accessed | tf_op | source)
XLA Modules:
  0.0 321.7 jit_solution(15642920557585341901)
XLA Ops:
  0.6 2.3 fusion.14
  3.0 20.2 %copy.5 = bf16[5,1088,1080]{2,1,0:T(8,128)(2,1)} copy(bf16[5,1088,1080]{1,2,0:T(8,128)(2,1)} %bitcast.29) | data formatting | bytes 23500800 | tf_op jit(solution)/shard_map/transpose | solution.py:305
  23.2 94.9 %strip_totals.1 = f32[5,136,1080]{2,1,0:T(8,128)} custom-call(bf16[5,4,2,136,1080]{4,3,2,1,0:T(8,128)(2,1)} %bitcast.28), custom_call_target="tpu_custom_call" | custom-call | tf_op jit(solution)/shard_map/strip_totals/pallas_call | solution.py:184
  118.0 17.7 %fusion.10 = f32[5,136,1080]{2,1,0:T(8,128)S(1)} fusion(f32[5,136,1080]{2,1,0:T(8,128)} %strip_totals.1, f32[1080]{0:T(1024)S(1)} %fusion.14, pred[1080]{0:T(1024)(128)(4,1)S(1)} %iota_compare_fusion), kind=kOutput, calls=%fused_computation.13 | convolution fusion | flops 9529056256 | bytes 5880600 | tf_op jit(solution)/shard_map/chv,wv->chw/dot_general | solution.py:310
  135.8 0.0 copy-start.1
  135.8 1.7 copy-done.1
  137.4 1.5 fusion.56
  138.9 0.0 copy-start
  138.9 2.7 collective-permute-start
  141.6 1.3 collective-permute-start.1
  143.0 0.2 fusion.37
  143.2 22.5 %collective-permute-done = f32[5,48,1080]{2,1,0:T(8,128)} collective-permute-done((f32[5,48,1080]{2,1,0:T(8,128)}, f32[5,48,1080]{2,1,0:T(8,128)}, u32[]{:S(2)}, u32[]{:S(2)}) %collective-permute-start) | collective-permute-done | bytes 1036832 | tf_op jit(solution)/shard_map/ppermute | solution.py:313
  165.7 0.0 collective-permute-done.1
  165.7 7.7 %fusion.16 = f32[5,136,1080]{2,1,0:T(8,128)} fusion(f32[5,48,1080]{2,1,0:T(8,128)} %collective-permute-done.1, f32[5,136,1080]{2,1,0:T(8,128)} %copy-done.1, f32[5,48,1080]{2,1,0:T(8,128)} %collective-permute-done, f32[136]{0:T(256)S(1)} %fusion.37, f32[232]{0:T(256)S(1)} %iota_add_fusion, f32[136]{0:T(256)S(1)} %iota_add_fusion.1, ...), kind=kOutput, calls=%fused_computation.20 | convolution fusion | flops 2047390720 | bytes 7951280 | tf_op jit(solution)/shard_map/hu,cuw->chw/dot_general | solution.py:321
  173.4 2.9 collective-permute-start.2
  176.3 0.0 copy-done
  176.4 0.0 copy-start.2
  176.4 1.9 multiply_bitcast_fusion
  178.2 2.1 collective-permute-done.2
  180.3 0.0 copy-done.2
  180.3 4.6 %select_bitcast_fusion = (f32[136,5,1080]{2,0,1:T(8,128)}, bf16[5,136,1080]{2,1,0:T(8,128)(2,1)}) fusion(f32[5,136,1080]{2,1,0:T(8,128)} %fusion.16, f32[5,136,1080]{2,1,0:T(8,128)} %collective-permute-done.2, pred[]{:T(512)S(6)} %eq.3, bf16[136,5,1080]{2,0,1:T(8,128)(2,1)S(1)} %copy-done.2), kind=kLoop, calls=%fused_computation.23 | loop fusion | flops 2937600 | bytes 11750401 | tf_op jit(solution)/shard_map/transpose | solution.py:329
  184.9 78.6 %gathered.1 = bf16[5,4,2,136,1080]{4,3,2,1,0:T(8,128)(2,1)} custom-call(bf16[5,136,1080]{2,1,0:T(8,128)(2,1)} %get-tuple-element.4.own_ref), custom_call_target="tpu_custom_call" | custom-call | tf_op jit(solution)/shard_map/gathered/pallas_call | solution.py:288
  263.5 14.3 %bitcast_convert_fusion = f32[5,1088,1080]{2,1,0:T(8,128)} fusion(bf16[5,4,2,136,1080]{4,3,2,1,0:T(8,128)(2,1)} %gathered.1), kind=kLoop, calls=%fused_computation.1 | loop fusion | flops 5875200 | bytes 35251200 | tf_op jit(solution)/shard_map/convert_element_type | solution.py:328
  277.7 26.2 %copy.6 = f32[5,1088,1080]{1,2,0:T(8,128)} copy(f32[5,1088,1080]{2,1,0:T(8,128)} %bitcast_convert_fusion) | data formatting | bytes 47001600 | tf_op jit(solution)/shard_map/convert_element_type | solution.py:328
  303.9 17.8 %fusion = bf16[1,1088,5,1080]{1,3,2,0:T(8,128)(2,1)} fusion(f32[5,1088,1080]{1,2,0:T(8,128)} %copy.6, bf16[1,1088,5,1080]{1,3,2,0:T(8,128)(2,1)} %param.2), kind=kLoop, calls=%fused_computation.2 | loop fusion | flops 17625600 | bytes 47001600 | tf_op jit(solution)/shard_map/broadcast_in_dim | solution.py:330
  (4 shorter events, 0.0 us)
Async XLA Ops:
  135.8 1.7 copy-start.1
  138.9 37.4 %copy-start = (f32[5,136,1080]{2,1,0:T(8,128)S(1)}, f32[5,136,1080]{2,1,0:T(8,128)}, u32[]{:S(2)}) copy-start(f32[5,136,1080]{2,1,0:T(8,128)} %strip_totals.1) | copy-start | bytes 8812804
  138.9 26.8 %collective-permute-start = (f32[5,48,1080]{2,1,0:T(8,128)}, f32[5,48,1080]{2,1,0:T(8,128)}, u32[]{:S(2)}, u32[]{:S(2)}) collective-permute-start(f32[5,48,1080]{2,1,0:T(8,128)} %get-tuple-element.5), channel_id=1, source_target_pairs={{0,3},{3,4},{4,7},{7,8},{8,11},{11,12},{12,15},{16,19},{19,20},{20... | collective-permute-start | bytes 3110408 | tf_op jit(solution)/shard_map/ppermute | solution.py:313
  141.6 24.1 %collective-permute-start.1 = (f32[5,48,1080]{2,1,0:T(8,128)}, f32[5,48,1080]{2,1,0:T(8,128)}, u32[]{:S(2)}, u32[]{:S(2)}) collective-permute-start(f32[5,48,1080]{2,1,0:T(8,128)} %get-tuple-element.6), channel_id=1, source_target_pairs={{3,0},{4,3},{7,4},{8,7},{11,8},{12,11},{15,12},{19,16},{20,19},{23... | collective-permute-start | bytes 3110408 | tf_op jit(solution)/shard_map/ppermute | solution.py:314
  173.4 6.9 %collective-permute-start.2 = (f32[5,136,1080]{2,1,0:T(8,128)}, f32[5,136,1080]{2,1,0:T(8,128)}, u32[]{:S(2)}, u32[]{:S(2)}) collective-permute-start(f32[5,136,1080]{2,1,0:T(8,128)} %fusion.16), channel_id=1, source_target_pairs={{0,1},{3,2},{4,5},{7,6},{8,9},{11,10},{12,13},{15,14},{16,17},{19,... | collective-permute-start | bytes 8812808 | tf_op jit(solution)/shard_map/ppermute | solution.py:326
  176.4 3.9 %copy-start.2 = (bf16[136,5,1080]{2,0,1:T(8,128)(2,1)S(1)}, bf16[136,5,1080]{2,0,1:T(8,128)(2,1)}, u32[]{:S(2)}) copy-start(bf16[136,5,1080]{2,0,1:T(8,128)(2,1)} %param.3) | copy-start | bytes 4406404

commit v2 on v1

--- a/solution.py
+++ b/solution.py
@@ -1,4 +1,3 @@
-import functools
 import jax
 import jax.numpy as jnp
 from jax import lax
@@ -9,6 +8,7 @@
 SIGMA = 16
 RADIUS = 48
 ROWS = 8
+COLUMNS = lax.Precision.HIGH
 MESH = pl.DeviceIdType.MESH
 LINK = jnp.bfloat16
 
@@ -55,9 +55,11 @@
     return {"strip": strip, "plate": plate}
 
 
-def greet(nz, strip, plate, y, z):
+def greet(nz, strip, plate, y, z, halo=False):
     barrier = pltpu.get_barrier_semaphore()
     partners = [at(strip, 1 - plate), at(z * 2 + 1 - y, plate)]
+    if halo:
+        partners += [at(lax.rem(strip + d, nz * 2), 1 - plate) for d in (1, nz * 2 - 1)]
     partners += [at(lax.rem(z + d, nz) * 2 + y, plate) for d in range(1, nz)]
     for partner in partners:
         pl.semaphore_signal(barrier, inc=1, device_id=partner, device_id_type=MESH)
@@ -65,12 +67,15 @@
 
 
 def reduce_kernel(x_ref, out_ref, mine, sib, pair, ybuf, zsend, zbuf, total,
-                  load_sem, sib_send, sib_recv, y_send, y_recv, z_send, z_recv, t_send, t_recv, o_sem):
-    channels, nz, _, rows, _ = x_ref.shape
+                  load_sem, sib_send, sib_recv, y_send, y_recv, z_send, z_recv, t_send, t_recv, h_send, h_recv, o_sem):
+    channels, nz, _, rows, width = x_ref.shape
     strip, plate, y, z = where_am_i()
     active = y == plate
     sibling = at(strip, 1 - plate)
-    greet(nz, strip, plate, y, z)
+    strips = nz * 2
+    inner = pl.ds(RADIUS, rows)
+    has_before, has_after = strip >= 1, strip + 1 < strips
+    greet(nz, strip, plate, y, z, halo=True)
 
     def load(c):
         return pltpu.make_async_copy(x_ref.at[c, :, plate], mine.at[c], load_sem.at[c])
@@ -89,6 +94,17 @@
         return pltpu.make_async_remote_copy(
             zsend.at[c, d], zbuf.at[c, d], z_send.at[c, d], z_recv.at[c, d],
             device_id=at(lax.rem(z + d, nz) * 2 + y, plate), device_id_type=MESH)
+
+    def halo_up(c):
+        return pltpu.make_async_remote_copy(
+            total.at[c, pl.ds(rows, RADIUS)], total.at[c, pl.ds(0, RADIUS)], h_send.at[c, 0], h_recv.at[c, 0],
+            device_id=at(lax.rem(strip + 1, strips), 1 - plate), device_id_type=MESH)
+
+    def halo_down(c):
+        return pltpu.make_async_remote_copy(
+            total.at[c, inner].at[pl.ds(0, RADIUS)], total.at[c, pl.ds(RADIUS + rows, RADIUS)],
+            h_send.at[c, 1], h_recv.at[c, 1],
+            device_id=at(lax.rem(strip + strips - 1, strips), 1 - plate), device_id_type=MESH)
 
     def share(c):
         return pltpu.make_async_remote_copy(
@@ -138,7 +154,7 @@
                 along(c, d).start()
 
             for r in range(0, rows, ROWS):
-                total[c, pl.ds(r, ROWS), :] = summed(z, r)
+                total[c, pl.ds(RADIUS + r, ROWS), :] = summed(z, r)
 
         @pl.loop(0, channels)
         def _(c):
@@ -148,16 +164,41 @@
 
             for r in range(0, rows, ROWS):
                 at_r = pl.ds(r, ROWS)
-                value = total[c, at_r, :]
+                value = total[c, pl.ds(RADIUS + r, ROWS), :]
                 for d in range(1, nz):
                     value = value + 4.0 * decoded(zbuf[c, d, at_r, :])
-                total[c, at_r, :] = value
+                total[c, pl.ds(RADIUS + r, ROWS), :] = value
+            pl.when(has_after)(lambda: halo_up(c).start())
+            pl.when(has_before)(lambda: halo_down(c).start())
+
+        outside = jnp.zeros((RADIUS, width), jnp.float32)
+
+        @pl.loop(0, channels)
+        def _(c):
+            @pl.when(has_before)
+            def _():
+                halo_up(c).wait_recv()
+
+            @pl.when(jnp.logical_not(has_before))
+            def _():
+                total[c, pl.ds(0, RADIUS), :] = outside
+
+            @pl.when(has_after)
+            def _():
+                halo_down(c).wait_recv()
+
+            @pl.when(jnp.logical_not(has_after))
+            def _():
+                total[c, pl.ds(RADIUS + rows, RADIUS), :] = outside
+
             share(c).start()
             store(c).start()
 
         @pl.loop(0, channels)
         def _(c):
             share(c).wait_send()
+            pl.when(has_after)(lambda: halo_up(c).wait_send())
+            pl.when(has_before)(lambda: halo_down(c).wait_send())
 
             @pl.loop(1, nz)
             def _(d):
@@ -183,16 +224,17 @@
     dma = pltpu.SemaphoreType.DMA
     return pl.pallas_call(
         reduce_kernel,
-        out_shape=jax.ShapeDtypeStruct((channels, rows, width), jnp.float32),
+        out_shape=jax.ShapeDtypeStruct((channels, rows + 2 * RADIUS, width), jnp.float32),
         in_specs=[pl.BlockSpec(memory_space=pl.ANY)],
         out_specs=pl.BlockSpec(memory_space=pl.ANY),
         scratch_shapes=[
             pltpu.VMEM(part, x.dtype), pltpu.VMEM(part, x.dtype),
             pltpu.VMEM(part, LINK), pltpu.VMEM(part, LINK),
             pltpu.VMEM(part, LINK), pltpu.VMEM(part, LINK),
-            pltpu.VMEM((channels, rows, width), jnp.float32),
+            pltpu.VMEM((channels, rows + 2 * RADIUS, width), jnp.float32),
             dma((channels,)), dma((channels,)), dma((channels,)), dma((channels,)), dma((channels,)),
-            dma((channels, nz)), dma((channels, nz)), dma((channels,)), dma((channels,)), dma((channels,)),
+            dma((channels, nz)), dma((channels, nz)), dma((channels,)), dma((channels,)),
+            dma((channels, 2)), dma((channels, 2)), dma((channels,)),
         ],
         compiler_params=pltpu.CompilerParams(
             collective_id=0, has_side_effects=True, vmem_limit_bytes=56 * 2**20),
@@ -296,38 +338,48 @@
     )(own)
 
 
+def divide_kernel(field_ref, illum_ref, out_ref):
+    illum = jnp.transpose(illum_ref[0]).astype(jnp.float32)
+    out_ref[0] = (field_ref[0].astype(jnp.float32) / illum).astype(out_ref.dtype)
+
+
+def divided(field, illum):
+    channels, width, height = field.shape
+    wide = 256
+    upright = pl.BlockSpec((1, wide, height), lambda c, w: (c, w, 0))
+    return pl.pallas_call(
+        divide_kernel,
+        grid=(channels, pl.cdiv(width, wide)),
+        out_shape=jax.ShapeDtypeStruct(field.shape, field.dtype),
+        in_specs=[upright, pl.BlockSpec((1, height, wide), lambda c, w: (c, 0, w))],
+        out_specs=upright,
+        compiler_params=pltpu.CompilerParams(vmem_limit_bytes=40 * 2**20),
+        name="divided",
+    )(field, illum)
+
+
 def on_grid(fields, flat_gain):
     _, height, channels, width = fields.shape
     strips = lax.axis_size("strip")
     nz = strips // 2
     strip_rows = height // strips
-    both = ("strip", "plate")
     x = jnp.transpose(fields[0], (1, 0, 2))
-    total = strip_totals(x.reshape(channels, nz, 2, strip_rows, width))
-    mean_field = total / (strips * 2)
-    col_index = jnp.arange(width, dtype=jnp.float32)
-    col_kernel = gauss_weights(col_index, col_index, float(width))
-    smooth_cols = jnp.einsum("chv,wv->chw", mean_field, col_kernel, precision=lax.Precision.HIGHEST)
-    up = [(i * 2 + i % 2, (i + 1) * 2 + (i + 1) % 2) for i in range(strips - 1)]
-    down = [(j, i) for i, j in up]
-    before = lax.ppermute(smooth_cols[:, strip_rows - RADIUS:], both, up)
-    after = lax.ppermute(smooth_cols[:, :RADIUS], both, down)
-    padded = jnp.concatenate([before, smooth_cols, after], axis=1)
-    strip = lax.axis_index("strip")
-    first_row = (strip * strip_rows).astype(jnp.float32)
+    padded = strip_totals(x.reshape(channels, nz, 2, strip_rows, width)) / (strips * 2)
+    mean_field = padded[:, RADIUS:RADIUS + strip_rows]
+    first_row = (lax.axis_index("strip") * strip_rows).astype(jnp.float32)
     out_index = first_row + jnp.arange(strip_rows, dtype=jnp.float32)
     in_index = first_row - RADIUS + jnp.arange(strip_rows + 2 * RADIUS, dtype=jnp.float32)
     row_kernel = gauss_weights(out_index, in_index, float(height))
-    illumination = jnp.einsum("hu,cuw->chw", row_kernel, padded, precision=lax.Precision.HIGHEST)
+    smooth_rows = jnp.einsum("hu,cuw->chw", row_kernel, padded, precision=lax.Precision.HIGHEST)
+    col_index = jnp.arange(width, dtype=jnp.float32)
+    col_kernel = gauss_weights(col_index, col_index, float(width))
+    illumination = jnp.einsum("chv,wv->chw", smooth_rows, col_kernel, precision=COLUMNS)
     gain = jnp.transpose(flat_gain, (1, 0, 2)).astype(jnp.float32)
     illum_round = (illumination * gain).astype(jnp.bfloat16)
     everywhere = gathered(illum_round, nz).reshape(channels, height, width)
-    twins = [(i * 2 + i % 2, i * 2 + 1 - i % 2) for i in range(strips)]
-    twin = lax.ppermute(illumination, both, twins)
-    illumination = jnp.where(lax.rem(strip, 2) == lax.axis_index("plate"), illumination, twin)
-    corrected = (x.astype(jnp.float32) / everywhere.astype(jnp.float32)).astype(jnp.bfloat16)
+    corrected = divided(jnp.transpose(fields[0], (1, 2, 0)), everywhere)
     back = lambda a: jnp.transpose(a, (1, 0, 2))
-    return (back(corrected)[None], back(illumination), back(mean_field))
+    return (jnp.transpose(corrected, (2, 0, 1))[None], back(illumination), back(mean_field))
 
 
 def on_device(fields, flat_gain):

time: 324 us -> 253 us (0.78)
  other arithmetic: 41.1 us -> 2.94 us
  Pallas kernels: 173 us -> 205 us
  waiting for transfers between devices: 24.6 us -> 0 us
  local copies, waits for them, and re-layouts: 49.5 us -> 26.7 us
  matrix products: 25.5 us -> 16.7 us
  starting transfers between devices: 6.92 us -> 0 us
    convert_element_type x1 -> x0, local copies, waits for them, and re-layouts: 26.2 us -> none  [on_grid(): everywhere.astype(jnp.float32)]
    ppermute x3 -> x0, waiting for transfers between devices: 24.6 us -> none  [the longest x1 22.5 us: on_grid(): before = lax.ppermute(smooth_cols[:, strip_rows - RADIUS:], both, up)]
    pallas_call x0 -> x1, Pallas kernels: none -> 20.4 us  [divided(): pl.pallas_call(divide_kernel, grid=(channels, pl.cdiv(width, wide)), out_...]
    broadcast_in_dim x1 -> x0, other arithmetic: 17.8 us -> none  [on_grid(): return (back(corrected)[None], back(illumination), back(mean_field))]
    convert_element_type x1 -> x0, other arithmetic: 14.3 us -> none  [on_grid(): everywhere.astype(jnp.float32)]
    pallas_call x1, Pallas kernels: 94.9 us -> 107 us  [strip_totals(): pl.pallas_call(reduce_kernel, out_shape=jax.ShapeDtypeStruct((channels, r...]
    dot_general x1, matrix products: 17.7 us -> 10.2 us  [on_grid(): jnp.einsum('chv,wv->chw', smooth_rows, col_kernel, precision=COLUMNS)]
    ppermute x3 -> x0, starting transfers between devices: 6.92 us -> none  [the longest x1 2.93 us: on_grid(): twin = lax.ppermute(illumination, both, twins)]
  transfers between devices with their start and end apart: 3 -> 0, of which waited for: 2 -> 0; matrix products, arithmetic and copies ran while one was open for 1% -> 0% of each run, Pallas kernels for 0% -> 0%
where the time goes in v2:
time: 253 us; the launch traced here: 252 us
  Pallas kernels  205 us (81%)
  local copies, waits for them, and re-layouts  26.7 us (11%)
  matrix products  16.7 us (7%)
  other arithmetic  2.94 us (1%)
    pallas_call x1, Pallas kernels, strip_totals(): pl.pallas_call(reduce_kernel, out_shape=jax.ShapeDtypeStruct((channels, r...  107 us
    pallas_call x1, Pallas kernels, gathered(): pl.pallas_call(gather_kernel, out_shape=jax.ShapeDtypeStruct((channels, n...  78.2 us
    pallas_call x1, Pallas kernels, divided(): pl.pallas_call(divide_kernel, grid=(channels, pl.cdiv(width, wide)), out_...  20.4 us
    transpose x1, local copies, waits for them, and re-layouts, on_grid(): x = jnp.transpose(fields[0], (1, 0, 2))  20.2 us
    dot_general x1, matrix products, on_grid(): jnp.einsum('chv,wv->chw', smooth_rows, col_kernel, precision=COLUMNS)  10.2 us
    dot_general x1, matrix products, on_grid(): jnp.einsum('hu,cuw->chw', row_kernel, padded, precision=lax.Precision.HIG...  6.53 us

profile of v2, /device:TPU:0, one launch (start us, length us, event | category | flops | bytes accessed | tf_op | source)
XLA Modules:
  0.0 252.3 jit_solution(3757192161929596561)
XLA Ops:
  0.7 0.2 fusion.25
  0.9 2.3 fusion.7
  3.3 20.2 %copy.7 = bf16[5,1088,1080]{2,1,0:T(8,128)(2,1)} copy(bf16[5,1088,1080]{1,2,0:T(8,128)(2,1)} %bitcast.28) | data formatting | bytes 23500800 | tf_op jit(solution)/shard_map/transpose | solution.py:366
  23.4 106.5 %strip_totals.1 = f32[5,232,1080]{2,1,0:T(8,128)} custom-call(bf16[5,4,2,136,1080]{4,3,2,1,0:T(8,128)(2,1)} %bitcast.31), custom_call_target="tpu_custom_call" | custom-call | tf_op jit(solution)/shard_map/strip_totals/pallas_call | solution.py:225
  130.0 0.0 copy-start.1
  130.0 6.5 %convolution_bitcast_fusion = f32[5,136,1080]{2,1,0:T(8,128)S(1)} fusion(f32[136]{0:T(256)S(1)} %fusion.25, f32[232]{0:T(256)S(1)} %iota_add_fusion, f32[136]{0:T(256)S(1)} %iota_add_fusion.1, pred[232]{0:T(512)(128)(4,1)S(1)} %get-tuple-element.5, pred[232]{0:T(512)(128)(4,1)S(1)} %get-tuple-element.6, f32[5,232,1080]{2,1,0:T(8,128)} %strip_totals.1), kind=kOutput, calls=%fused_computation.11 | convolution fusion | flops 2046137856 | bytes 7951280 | tf_op jit(solution)/shard_map/hu,cuw->chw/dot_general | solution.py:373
  136.5 0.0 copy-done.1
  136.6 0.3 broadcast_multiply_fusion
  136.9 0.0 copy-start.2
  136.9 1.9 slice_bitcast_fusion
  138.8 0.1 copy-done.2
  138.9 10.2 %fusion.9 = (bf16[5,136,1080]{2,1,0:T(8,128)(2,1)}, f32[5,136,1080]{2,1,0:T(8,128)}) fusion(bf16[136,5,1080]{2,0,1:T(8,128)(2,1)S(1)} %copy-done.2, f32[5,136,1080]{2,1,0:T(8,128)S(1)} %convolution_bitcast_fusion, f32[1080]{0:T(1024)S(1)} %fusion.7, pred[1080]{0:T(1024)(128)(4,1)S(1)} %iota_compare_fusion), kind=kOutput, calls=%fused_computation.14 | convolution fusion | flops 4771612672 | bytes 8818200 | tf_op jit(solution)/shard_map/chv,wv->chw/dot_general | solution.py:376
  149.1 78.2 %gathered.1 = bf16[5,4,2,136,1080]{4,3,2,1,0:T(8,128)(2,1)} custom-call(bf16[5,136,1080]{2,1,0:T(8,128)(2,1)} %get-tuple-element.3.own_ref), custom_call_target="tpu_custom_call" | custom-call | tf_op jit(solution)/shard_map/gathered/pallas_call | solution.py:330
  227.3 0.0 copy-start
  227.3 4.5 %copy-done = bf16[1,1088,5,1080]{1,3,2,0:T(8,128)(2,1)S(1)} copy-done((bf16[1,1088,5,1080]{1,3,2,0:T(8,128)(2,1)S(1)}, bf16[1,1088,5,1080]{1,3,2,0:T(8,128)(2,1)}, u32[]{:S(2)}) %copy-start) | copy-done | bytes 11750424
  231.9 20.4 %divided.1 = bf16[5,1080,1088]{2,1,0:T(8,128)(2,1)} custom-call(bf16[5,1080,1088]{2,1,0:T(8,128)(2,1)S(1)} %bitcast.29, bf16[5,1088,1080]{2,1,0:T(8,128)(2,1)} %bitcast.30), custom_call_target="tpu_custom_call" | custom-call | tf_op jit(solution)/shard_map/divided/pallas_call | solution.py:350
  (4 shorter events, 0.0 us)
Async XLA Ops:
  130.0 6.5 %copy-start.1 = (f32[5,232,1080]{2,1,0:T(8,128)S(1)}, f32[5,232,1080]{2,1,0:T(8,128)}, u32[]{:S(2)}) copy-start(f32[5,232,1080]{2,1,0:T(8,128)} %strip_totals.1) | copy-start | bytes 15033604
  136.9 2.0 copy-start.2
  227.3 4.5 %copy-start = (bf16[1,1088,5,1080]{1,3,2,0:T(8,128)(2,1)S(1)}, bf16[1,1088,5,1080]{1,3,2,0:T(8,128)(2,1)}, u32[]{:S(2)}) copy-start(bf16[1,1088,5,1080]{1,3,2,0:T(8,128)(2,1)} %param.2) | copy-start | bytes 35251204

commit v3 on v2

--- a/solution.py
+++ b/solution.py
@@ -8,6 +8,7 @@
 SIGMA = 16
 RADIUS = 48
 ROWS = 8
+WIDE = 256
 COLUMNS = lax.Precision.HIGH
 MESH = pl.DeviceIdType.MESH
 LINK = jnp.bfloat16
@@ -66,33 +67,32 @@
     pl.semaphore_wait(barrier, len(partners))
 
 
-def reduce_kernel(x_ref, out_ref, mine, sib, pair, ybuf, zsend, zbuf, total,
+def reduce_kernel(x_ref, out_ref, raw, turned, sib, outbox, ybuf, zbuf, total,
                   load_sem, sib_send, sib_recv, y_send, y_recv, z_send, z_recv, t_send, t_recv, h_send, h_recv, o_sem):
-    channels, nz, _, rows, width = x_ref.shape
+    channels, nz, _, rows, width = turned.shape
     strip, plate, y, z = where_am_i()
     active = y == plate
     sibling = at(strip, 1 - plate)
     strips = nz * 2
     inner = pl.ds(RADIUS, rows)
     has_before, has_after = strip >= 1, strip + 1 < strips
-    greet(nz, strip, plate, y, z, halo=True)
 
     def load(c):
-        return pltpu.make_async_copy(x_ref.at[c, :, plate], mine.at[c], load_sem.at[c])
+        return pltpu.make_async_copy(x_ref.at[c], raw.at[lax.rem(c, 2)], load_sem.at[c])
 
     def to_sibling(c):
         return pltpu.make_async_remote_copy(
-            x_ref.at[c, :, 1 - plate], sib.at[c], sib_send.at[c], sib_recv.at[c],
+            turned.at[c, :, 1 - plate], sib.at[c], sib_send.at[c], sib_recv.at[c],
             device_id=sibling, device_id_type=MESH)
 
     def across(c):
         return pltpu.make_async_remote_copy(
-            pair.at[c], ybuf.at[c], y_send.at[c], y_recv.at[c],
+            outbox.at[c], ybuf.at[c], y_send.at[c], y_recv.at[c],
             device_id=at(z * 2 + 1 - y, plate), device_id_type=MESH)
 
     def along(c, d):
         return pltpu.make_async_remote_copy(
-            zsend.at[c, d], zbuf.at[c, d], z_send.at[c, d], z_recv.at[c, d],
+            outbox.at[c, d], zbuf.at[c, d], z_send.at[c, d], z_recv.at[c, d],
             device_id=at(lax.rem(z + d, nz) * 2 + y, plate), device_id_type=MESH)
 
     def halo_up(c):
@@ -114,14 +114,24 @@
     def store(c):
         return pltpu.make_async_copy(total.at[c], out_ref.at[c], o_sem.at[c])
 
+    def turn(c):
+        load(c).wait()
+        for w in range(0, width, WIDE):
+            wide = min(WIDE, width - w)
+            block = jnp.transpose(raw[lax.rem(c, 2), pl.ds(w, wide), :])
+            for k in range(nz * 2):
+                turned[c, k // 2, k % 2, :, pl.ds(w, wide)] = block[k * rows:(k + 1) * rows]
+        pl.when(c + 2 < channels)(lambda: load(c + 2).start())
+        to_sibling(c).start()
+
+    load(0).start()
+    load(1).start()
+    greet(nz, strip, plate, y, z, halo=True)
+    turn(0)
+
     @pl.loop(0, channels)
     def _(c):
-        load(c).start()
-        to_sibling(c).start()
-
-    @pl.loop(0, channels)
-    def _(c):
-        load(c).wait()
+        pl.when(c + 1 < channels)(lambda: turn(c + 1))
         to_sibling(c).wait_recv()
 
         @pl.when(jnp.logical_not(active))
@@ -130,8 +140,8 @@
             def _(k):
                 for r in range(0, rows, ROWS):
                     at_r = pl.ds(r, ROWS)
-                    value = mine[c, k, at_r, :].astype(jnp.float32) + sib[c, k, at_r, :].astype(jnp.float32)
-                    pair[c, k, at_r, :] = coded(value * 0.5)
+                    value = turned[c, k, plate, at_r, :].astype(jnp.float32) + sib[c, k, at_r, :].astype(jnp.float32)
+                    outbox[c, k, at_r, :] = coded(value * 0.5)
 
             across(c).start()
 
@@ -143,14 +153,14 @@
 
             def summed(k, r):
                 at_r = pl.ds(r, ROWS)
-                value = mine[c, k, at_r, :].astype(jnp.float32) + sib[c, k, at_r, :].astype(jnp.float32)
+                value = turned[c, k, plate, at_r, :].astype(jnp.float32) + sib[c, k, at_r, :].astype(jnp.float32)
                 return value + 2.0 * decoded(ybuf[c, k, at_r, :])
 
             @pl.loop(1, nz)
             def _(d):
                 k = lax.rem(z + d, nz)
                 for r in range(0, rows, ROWS):
-                    zsend[c, d, pl.ds(r, ROWS), :] = coded(summed(k, r) * 0.25)
+                    outbox[c, d, pl.ds(r, ROWS), :] = coded(summed(k, r) * 0.25)
                 along(c, d).start()
 
             for r in range(0, rows, ROWS):
@@ -218,8 +228,9 @@
         store(c).wait()
 
 
-def strip_totals(x):
-    channels, nz, _, rows, width = x.shape
+def strip_totals(x, nz):
+    channels, width, height = x.shape
+    rows = height // (nz * 2)
     part = (channels, nz, rows, width)
     dma = pltpu.SemaphoreType.DMA
     return pl.pallas_call(
@@ -228,9 +239,8 @@
         in_specs=[pl.BlockSpec(memory_space=pl.ANY)],
         out_specs=pl.BlockSpec(memory_space=pl.ANY),
         scratch_shapes=[
-            pltpu.VMEM(part, x.dtype), pltpu.VMEM(part, x.dtype),
-            pltpu.VMEM(part, LINK), pltpu.VMEM(part, LINK),
-            pltpu.VMEM(part, LINK), pltpu.VMEM(part, LINK),
+            pltpu.VMEM((2, width, height), x.dtype), pltpu.VMEM((channels, nz, 2, rows, width), x.dtype),
+            pltpu.VMEM(part, x.dtype), pltpu.VMEM(part, LINK), pltpu.VMEM(part, LINK), pltpu.VMEM(part, LINK),
             pltpu.VMEM((channels, rows + 2 * RADIUS, width), jnp.float32),
             dma((channels,)), dma((channels,)), dma((channels,)), dma((channels,)), dma((channels,)),
             dma((channels, nz)), dma((channels, nz)), dma((channels,)), dma((channels,)),
@@ -345,7 +355,7 @@
 
 def divided(field, illum):
     channels, width, height = field.shape
-    wide = 256
+    wide = WIDE
     upright = pl.BlockSpec((1, wide, height), lambda c, w: (c, w, 0))
     return pl.pallas_call(
         divide_kernel,
@@ -363,8 +373,8 @@
     strips = lax.axis_size("strip")
     nz = strips // 2
     strip_rows = height // strips
-    x = jnp.transpose(fields[0], (1, 0, 2))
-    padded = strip_totals(x.reshape(channels, nz, 2, strip_rows, width)) / (strips * 2)
+    x = jnp.transpose(fields[0], (1, 2, 0))
+    padded = strip_totals(x, nz) / (strips * 2)
     mean_field = padded[:, RADIUS:RADIUS + strip_rows]
     first_row = (lax.axis_index("strip") * strip_rows).astype(jnp.float32)
     out_index = first_row + jnp.arange(strip_rows, dtype=jnp.float32)
@@ -377,7 +387,7 @@
     gain = jnp.transpose(flat_gain, (1, 0, 2)).astype(jnp.float32)
     illum_round = (illumination * gain).astype(jnp.bfloat16)
     everywhere = gathered(illum_round, nz).reshape(channels, height, width)
-    corrected = divided(jnp.transpose(fields[0], (1, 2, 0)), everywhere)
+    corrected = divided(x, everywhere)
     back = lambda a: jnp.transpose(a, (1, 0, 2))
     return (jnp.transpose(corrected, (2, 0, 1))[None], back(illumination), back(mean_field))
 

time: 253 us -> 234 us (0.925)
  local copies, waits for them, and re-layouts: 26.7 us -> 6.55 us
    transpose x1 -> x0, local copies, waits for them, and re-layouts: 20.2 us -> none  [on_grid(): x = jnp.transpose(fields[0], (1, 0, 2))]
where the time goes in v3:
time: 234 us; the launch traced here: 233 us
  Pallas kernels  206 us (88%)
  matrix products  16.7 us (7%)
  local copies, waits for them, and re-layouts  6.55 us (3%)
  other arithmetic  2.94 us (1%)
    pallas_call x1, Pallas kernels, strip_totals(): pl.pallas_call(reduce_kernel, out_shape=jax.ShapeDtypeStruct((channels, r...  107 us
    pallas_call x1, Pallas kernels, gathered(): pl.pallas_call(gather_kernel, out_shape=jax.ShapeDtypeStruct((channels, n...  78.6 us
    pallas_call x1, Pallas kernels, divided(): pl.pallas_call(divide_kernel, grid=(channels, pl.cdiv(width, wide)), out_...  20.4 us
    dot_general x1, matrix products, on_grid(): jnp.einsum('chv,wv->chw', smooth_rows, col_kernel, precision=COLUMNS)  10.2 us
    dot_general x1, matrix products, on_grid(): jnp.einsum('hu,cuw->chw', row_kernel, padded, precision=lax.Precision.HIG...  6.53 us
    unnamed x6, local copies, waits for them, and re-layouts  4.69 us

profile of v3, /device:TPU:0, one launch (start us, length us, event | category | flops | bytes accessed | tf_op | source)
XLA Modules:
  0.0 233.1 jit_solution(7744529187643062823)
XLA Ops:
  0.7 0.2 fusion.25
  0.9 2.3 fusion.7
  3.3 107.2 %strip_totals.1 = f32[5,232,1080]{2,1,0:T(8,128)} custom-call(bf16[5,1080,1088]{2,1,0:T(8,128)(2,1)} %bitcast.25), custom_call_target="tpu_custom_call" | custom-call | tf_op jit(solution)/shard_map/strip_totals/pallas_call | solution.py:236
  110.4 0.0 copy-start.1
  110.4 6.5 %convolution_bitcast_fusion = f32[5,136,1080]{2,1,0:T(8,128)S(1)} fusion(f32[136]{0:T(256)S(1)} %fusion.25, f32[232]{0:T(256)S(1)} %iota_add_fusion, f32[136]{0:T(256)S(1)} %iota_add_fusion.1, pred[232]{0:T(512)(128)(4,1)S(1)} %get-tuple-element.5, pred[232]{0:T(512)(128)(4,1)S(1)} %get-tuple-element.6, f32[5,232,1080]{2,1,0:T(8,128)} %strip_totals.1), kind=kOutput, calls=%fused_computation.11 | convolution fusion | flops 2046137856 | bytes 7951280 | tf_op jit(solution)/shard_map/hu,cuw->chw/dot_general | solution.py:383
  117.0 0.0 copy-done.1
  117.0 0.3 broadcast_multiply_fusion
  117.3 0.0 copy-start.2
  117.3 1.9 slice_bitcast_fusion
  119.2 0.1 copy-done.2
  119.3 10.2 %fusion.9 = (bf16[5,136,1080]{2,1,0:T(8,128)(2,1)}, f32[5,136,1080]{2,1,0:T(8,128)}) fusion(bf16[136,5,1080]{2,0,1:T(8,128)(2,1)S(1)} %copy-done.2, f32[5,136,1080]{2,1,0:T(8,128)S(1)} %convolution_bitcast_fusion, f32[1080]{0:T(1024)S(1)} %fusion.7, pred[1080]{0:T(1024)(128)(4,1)S(1)} %iota_compare_fusion), kind=kOutput, calls=%fused_computation.14 | convolution fusion | flops 4771612672 | bytes 8818200 | tf_op jit(solution)/shard_map/chv,wv->chw/dot_general | solution.py:386
  129.5 78.6 %gathered.1 = bf16[5,4,2,136,1080]{4,3,2,1,0:T(8,128)(2,1)} custom-call(bf16[5,136,1080]{2,1,0:T(8,128)(2,1)} %get-tuple-element.3.own_ref), custom_call_target="tpu_custom_call" | custom-call | tf_op jit(solution)/shard_map/gathered/pallas_call | solution.py:340
  208.2 0.0 copy-start
  208.2 4.5 %copy-done = bf16[1,1088,5,1080]{1,3,2,0:T(8,128)(2,1)S(1)} copy-done((bf16[1,1088,5,1080]{1,3,2,0:T(8,128)(2,1)S(1)}, bf16[1,1088,5,1080]{1,3,2,0:T(8,128)(2,1)}, u32[]{:S(2)}) %copy-start) | copy-done | bytes 11750424
  212.7 20.4 %divided.1 = bf16[5,1080,1088]{2,1,0:T(8,128)(2,1)} custom-call(bf16[5,1080,1088]{2,1,0:T(8,128)(2,1)S(1)} %bitcast.26, bf16[5,1088,1080]{2,1,0:T(8,128)(2,1)} %bitcast.27), custom_call_target="tpu_custom_call" | custom-call | tf_op jit(solution)/shard_map/divided/pallas_call | solution.py:360
  (4 shorter events, 0.0 us)
Async XLA Ops:
  110.4 6.5 %copy-start.1 = (f32[5,232,1080]{2,1,0:T(8,128)S(1)}, f32[5,232,1080]{2,1,0:T(8,128)}, u32[]{:S(2)}) copy-start(f32[5,232,1080]{2,1,0:T(8,128)} %strip_totals.1) | copy-start | bytes 15033604
  117.3 2.0 copy-start.2
  208.2 4.5 %copy-start = (bf16[1,1088,5,1080]{1,3,2,0:T(8,128)(2,1)S(1)}, bf16[1,1088,5,1080]{1,3,2,0:T(8,128)(2,1)}, u32[]{:S(2)}) copy-start(bf16[1,1088,5,1080]{1,3,2,0:T(8,128)(2,1)} %param.2) | copy-start | bytes 35251204

commit v4 on v3

--- a/solution.py
+++ b/solution.py
@@ -355,7 +355,7 @@
 
 def divided(field, illum):
     channels, width, height = field.shape
-    wide = WIDE
+    wide = 384
     upright = pl.BlockSpec((1, wide, height), lambda c, w: (c, w, 0))
     return pl.pallas_call(
         divide_kernel,

time: 234 us -> 230 us (0.983)
  Pallas kernels: 206 us -> 203 us
    pallas_call x1, Pallas kernels: 20.4 us -> 17.2 us  [divided(): pl.pallas_call(divide_kernel, grid=(channels, pl.cdiv(width, wide)), out_...]
where the time goes in v4:
time: 230 us
  Pallas kernels  203 us (88%)
  matrix products  16.7 us (7%)
  local copies, waits for them, and re-layouts  6.55 us (3%)
  other arithmetic  2.94 us (1%)
    pallas_call x1, Pallas kernels, strip_totals(): pl.pallas_call(reduce_kernel, out_shape=jax.ShapeDtypeStruct((channels, r...  107 us
    pallas_call x1, Pallas kernels, gathered(): pl.pallas_call(gather_kernel, out_shape=jax.ShapeDtypeStruct((channels, n...  78.6 us
    pallas_call x1, Pallas kernels, divided(): pl.pallas_call(divide_kernel, grid=(channels, pl.cdiv(width, wide)), out_...  17.2 us
    dot_general x1, matrix products, on_grid(): jnp.einsum('chv,wv->chw', smooth_rows, col_kernel, precision=COLUMNS)  10.2 us
    dot_general x1, matrix products, on_grid(): jnp.einsum('hu,cuw->chw', row_kernel, padded, precision=lax.Precision.HIG...  6.53 us
    unnamed x6, local copies, waits for them, and re-layouts  4.69 us

profile of v4, /device:TPU:0, one launch (start us, length us, event | category | flops | bytes accessed | tf_op | source)
XLA Modules:
  0.0 229.9 jit_solution(18134811166108255393)
XLA Ops:
  0.7 0.2 fusion.25
  0.9 2.3 %fusion.7 = f32[1080]{0:T(1024)S(1)} fusion(pred[1080]{0:T(1024)(128)(4,1)S(1)} %iota_compare_fusion), kind=kLoop, calls=%fused_computation.9 | loop fusion | flops 10496520 | bytes 5400 | tf_op jit(solution)/shard_map/reduce_sum | solution.py:47
  3.3 107.2 %strip_totals.1 = f32[5,232,1080]{2,1,0:T(8,128)} custom-call(bf16[5,1080,1088]{2,1,0:T(8,128)(2,1)} %bitcast.25), custom_call_target="tpu_custom_call" | custom-call | tf_op jit(solution)/shard_map/strip_totals/pallas_call | solution.py:236
  110.4 0.0 copy-start.1
  110.4 6.5 %convolution_bitcast_fusion = f32[5,136,1080]{2,1,0:T(8,128)S(1)} fusion(f32[136]{0:T(256)S(1)} %fusion.25, f32[232]{0:T(256)S(1)} %iota_add_fusion, f32[136]{0:T(256)S(1)} %iota_add_fusion.1, pred[232]{0:T(512)(128)(4,1)S(1)} %get-tuple-element.5, pred[232]{0:T(512)(128)(4,1)S(1)} %get-tuple-element.6, f32[5,232,1080]{2,1,0:T(8,128)} %strip_totals.1), kind=kOutput, calls=%fused_computation.11 | convolution fusion | flops 2046137856 | bytes 7951280 | tf_op jit(solution)/shard_map/hu,cuw->chw/dot_general | solution.py:383
  117.0 0.0 copy-done.1
  117.0 0.3 broadcast_multiply_fusion
  117.3 0.0 copy-start.2
  117.3 1.9 slice_bitcast_fusion
  119.2 0.1 copy-done.2
  119.3 10.2 %fusion.9 = (bf16[5,136,1080]{2,1,0:T(8,128)(2,1)}, f32[5,136,1080]{2,1,0:T(8,128)}) fusion(bf16[136,5,1080]{2,0,1:T(8,128)(2,1)S(1)} %copy-done.2, f32[5,136,1080]{2,1,0:T(8,128)S(1)} %convolution_bitcast_fusion, f32[1080]{0:T(1024)S(1)} %fusion.7, pred[1080]{0:T(1024)(128)(4,1)S(1)} %iota_compare_fusion), kind=kOutput, calls=%fused_computation.14 | convolution fusion | flops 4771612672 | bytes 8818200 | tf_op jit(solution)/shard_map/chv,wv->chw/dot_general | solution.py:386
  129.5 78.6 %gathered.1 = bf16[5,4,2,136,1080]{4,3,2,1,0:T(8,128)(2,1)} custom-call(bf16[5,136,1080]{2,1,0:T(8,128)(2,1)} %get-tuple-element.3.own_ref), custom_call_target="tpu_custom_call" | custom-call | tf_op jit(solution)/shard_map/gathered/pallas_call | solution.py:340
  208.2 0.0 copy-start
  208.2 4.5 %copy-done = bf16[1,1088,5,1080]{1,3,2,0:T(8,128)(2,1)S(1)} copy-done((bf16[1,1088,5,1080]{1,3,2,0:T(8,128)(2,1)S(1)}, bf16[1,1088,5,1080]{1,3,2,0:T(8,128)(2,1)}, u32[]{:S(2)}) %copy-start) | copy-done | bytes 11750424
  212.7 17.2 %divided.1 = bf16[5,1080,1088]{2,1,0:T(8,128)(2,1)} custom-call(bf16[5,1080,1088]{2,1,0:T(8,128)(2,1)S(1)} %bitcast.26, bf16[5,1088,1080]{2,1,0:T(8,128)(2,1)} %bitcast.27), custom_call_target="tpu_custom_call" | custom-call | tf_op jit(solution)/shard_map/divided/pallas_call | solution.py:360
  (4 shorter events, 0.0 us)
Async XLA Ops:
  110.4 6.5 %copy-start.1 = (f32[5,232,1080]{2,1,0:T(8,128)S(1)}, f32[5,232,1080]{2,1,0:T(8,128)}, u32[]{:S(2)}) copy-start(f32[5,232,1080]{2,1,0:T(8,128)} %strip_totals.1) | copy-start | bytes 15033604
  117.3 2.0 copy-start.2
  208.2 4.5 %copy-start = (bf16[1,1088,5,1080]{1,3,2,0:T(8,128)(2,1)S(1)}, bf16[1,1088,5,1080]{1,3,2,0:T(8,128)(2,1)}, u32[]{:S(2)}) copy-start(bf16[1,1088,5,1080]{1,3,2,0:T(8,128)(2,1)} %param.2) | copy-start | bytes 35251204
